TPU v7x, 128 devices: a whole 4x4x4 slice. The times are simulated.
128 devices in a mesh: dp: 8 (over x, core), seq: 16 (over z, y).
Axes of the slice: x: 4, y: 4, z: 4, core: 2. Of those that a mesh axis runs over, the one named last changes fastest.
Arguments:
- queries: bfloat16 [8, 2048, 4096], P('dp', 'seq'), may hold values from -24 to 24
- keys: bfloat16 [8, 2048, 1024], P('dp', 'seq'), may hold values from -6 to 6
- values: bfloat16 [8, 2048, 1024], P('dp', 'seq'), may hold values from -48 to 48
- stem_kv: bfloat16 [8, 2, 4096, 1024], P('dp', None, 'seq'), may hold values from -48 to 48
- seg_ids: int32 [8, 2048], P('dp'), may hold values from 0 to 15, never falling along the last dimension, each value on 1 to 512 neighbouring positions
- seg_parent: int32 [8, 16], P('dp'), may hold values from 0 to 14, as said below
- stem_owner: int32 [8], replicated, may hold values from 0 to 7
Outputs:
- attended: bfloat16 [8, 2048, 4096], P('dp', 'seq')
Inputs may be any that keep to these rules, and one draw needn't show every extreme that they name: seg_parent[g, 0] = 0 and seg_parent[g, s] < s for s >= 1, so each pack's segments form a tree rooted at segment 0. Pack g attends to the stem stored by group stem_owner[g].
All inputs are finite; a program needn't handle non-finite values.
Results may differ from a plain program's by a relative error of at most 0.0088.
Values may be sent and summed in bfloat16 or wider, within the bound.
No kernel may reach another device: no remote copies, remote signals or barrier semaphores. Data moves between devices by JAX's collectives and lax.ppermute only.
A program may use at most 64 MiB of HBM per device.

v0:
```python
import math
import jax
import jax.numpy as jnp
import numpy as np
from jax import lax
from jax.sharding import PartitionSpec as P

H = 32
KVH = 8
HD = 128
STEM = 4096
SEGS = 16


def as_sent(value):

    def short(part):
        return part.astype(jnp.bfloat16) if part.dtype == jnp.float32 else part

    return jax.tree.map(short, value)


def rotary_table():
    halves = np.arange(0, HD, 2) / HD
    inverse = 1.0 / 500000.0**halves
    wavelen = 2.0 * np.pi / inverse
    smooth = (8192.0 / wavelen - 1.0) / 3.0
    blended = (1.0 - smooth) * inverse / 8.0 + smooth * inverse
    scaled = np.where(wavelen < 2048.0, inverse, np.where(wavelen > 8192.0, inverse / 8.0, blended))
    return jnp.asarray(scaled, dtype=jnp.float32)


def rotate(head_block, places):
    rotary = rotary_table()
    angles = places[:, None] * rotary[None, :]
    cosine = jnp.concatenate([jnp.cos(angles), jnp.cos(angles)], axis=1)[:, None, :]
    sine_full = jnp.concatenate([jnp.sin(angles), jnp.sin(angles)], axis=1)[:, None, :]
    widened = head_block.astype(jnp.float32)
    rolled = jnp.concatenate([-widened[..., HD // 2 :], widened[..., : HD // 2]], axis=-1)
    return (widened * cosine + rolled * sine_full).astype(jnp.bfloat16)


def ancestry(parents):
    seg_count = parents.shape[0]
    indices = jnp.arange(seg_count, dtype=jnp.int32)
    linked = (
        (indices[:, None] == indices[None, :]) | (parents[:, None] == indices[None, :])
    ).astype(jnp.float32)
    for sweep in range(max(1, (seg_count - 1).bit_length())):
        linked = (
            jnp.dot(
                linked, linked, precision=lax.Precision.HIGHEST, preferred_element_type=jnp.float32
            )
            > 0.5
        ).astype(jnp.float32)
    return linked


def token_places(seg_row, linked):
    seg_count = linked.shape[0]
    onehot = (seg_row[:, None] == jnp.arange(seg_count, dtype=jnp.int32)[None, :]).astype(
        jnp.float32
    )
    lengths = jnp.sum(onehot, axis=0)
    starts = jnp.cumsum(lengths) - lengths
    before = jnp.sum(linked * lengths[None, :], axis=1) - lengths
    token_ids = jnp.arange(seg_row.shape[0], dtype=jnp.int32).astype(jnp.float32)
    return (
        STEM
        + token_ids
        - jnp.sum(onehot * starts[None, :], axis=1)
        + jnp.sum(onehot * before[None, :], axis=1)
    )


def shards(queries, keys, values, stem_kv, seg_ids, seg_parent, stem_owner):
    tok_count = queries.shape[1]
    seq_count = lax.axis_size("seq")
    pack_len = tok_count * seq_count
    group_size = H // KVH
    local_heads = H // seq_count
    repeat = max(1, seq_count // KVH)
    kv_local = max(KVH, seq_count) // seq_count
    seg_row = seg_ids[0]
    linked = ancestry(seg_parent[0])
    places = token_places(seg_row, linked)
    own_places = lax.dynamic_slice_in_dim(places, lax.axis_index("seq") * tok_count, tok_count)
    q_rot = rotate(queries[0].reshape(tok_count, H, HD), own_places).reshape(tok_count, H * HD)
    k_rot = rotate(keys[0].reshape(tok_count, KVH, HD), own_places)
    k_wide = jnp.repeat(k_rot, repeat, axis=1).reshape(tok_count, repeat * KVH * HD)
    v_wide = jnp.repeat(values[0].reshape(tok_count, KVH, HD), repeat, axis=1).reshape(
        tok_count, repeat * KVH * HD
    )
    q_heads, k_heads, v_heads = (
        lax.all_to_all(q_rot, "seq", split_axis=1, concat_axis=0, tiled=True),
        lax.all_to_all(k_wide, "seq", split_axis=1, concat_axis=0, tiled=True),
        lax.all_to_all(v_wide, "seq", split_axis=1, concat_axis=0, tiled=True),
    )
    owner_group = lax.dynamic_index_in_dim(stem_owner, lax.axis_index("dp"), 0, keepdims=False)
    empty_block = jnp.zeros(stem_kv.shape[1:], jnp.bfloat16)
    incoming = lax.all_gather(stem_kv, "dp", axis=0, tiled=True)
    inside = (owner_group >= 0) & (owner_group < incoming.shape[0])
    chosen = lax.dynamic_index_in_dim(
        incoming, jnp.clip(owner_group, 0, incoming.shape[0] - 1), 0, keepdims=False
    )
    owned = jnp.where(inside, chosen, empty_block)
    stem_rows = owned.shape[1]
    stem_wide = jnp.repeat(owned.reshape(2, stem_rows, KVH, HD), repeat, axis=2).reshape(
        2, stem_rows, repeat * KVH * HD
    )
    stem_heads = lax.all_to_all(stem_wide, "seq", split_axis=2, concat_axis=1, tiled=True)
    stem_len = stem_heads.shape[1]
    key_sets = jnp.concatenate(
        [stem_heads[0].reshape(stem_len, kv_local, HD), k_heads.reshape(pack_len, kv_local, HD)],
        axis=0,
    )
    value_sets = jnp.concatenate(
        [stem_heads[1].reshape(stem_len, kv_local, HD), v_heads.reshape(pack_len, kv_local, HD)],
        axis=0,
    )
    onehot = (seg_row[:, None] == jnp.arange(SEGS, dtype=jnp.int32)[None, :]).astype(jnp.float32)
    reach_rows = jnp.dot(
        onehot, linked, precision=lax.Precision.HIGHEST, preferred_element_type=jnp.float32
    )
    qblock = math.gcd(512, pack_len)
    score_scale = HD ** (-0.5)
    token_ids = jnp.arange(pack_len, dtype=jnp.int32)

    def block_out(block_index):
        row_start = block_index * qblock
        reach_block = lax.dynamic_slice_in_dim(reach_rows, row_start, qblock)
        reach_mask = (
            jnp.dot(
                reach_block,
                onehot.T,
                precision=lax.Precision.HIGHEST,
                preferred_element_type=jnp.float32,
            )
            > 0.5
        )
        row_ids = row_start + jnp.arange(qblock, dtype=jnp.int32)
        visible = jnp.concatenate(
            [
                jnp.ones((qblock, stem_len), dtype=jnp.bool_),
                reach_mask & (token_ids[None, :] <= row_ids[:, None]),
            ],
            axis=1,
        )
        pieces = []
        for head_index in range(local_heads):
            kv_head = head_index // group_size
            query_rows = lax.dynamic_slice(q_heads, (row_start, head_index * HD), (qblock, HD))
            scores = (
                jnp.einsum(
                    "qd,kd->qk",
                    query_rows,
                    key_sets[:, kv_head],
                    preferred_element_type=jnp.float32,
                )
                * score_scale
            )
            masked = jnp.where(visible, scores, -jnp.inf)
            row_max = jnp.max(masked, axis=1, keepdims=True)
            exp_scores = jnp.exp(masked - row_max)
            totals = jnp.sum(exp_scores, axis=1, keepdims=True)
            mixed_sum = jnp.dot(
                exp_scores.astype(jnp.bfloat16),
                value_sets[:, kv_head],
                preferred_element_type=jnp.float32,
            )
            pieces.append((mixed_sum / totals).astype(jnp.bfloat16))
        return jnp.concatenate(pieces, axis=1)

    blocks = lax.map(block_out, jnp.arange(pack_len // qblock, dtype=jnp.int32))
    attended_heads = blocks.reshape(pack_len, local_heads * HD)
    back = lax.all_to_all(
        as_sent(attended_heads), "seq", split_axis=0, concat_axis=1, tiled=True
    ).astype(attended_heads.dtype)
    return back.reshape(1, tok_count, H * HD)


def solution(mesh):
    placed = (
        P("dp", "seq", None),
        P("dp", "seq", None),
        P("dp", "seq", None),
        P("dp", None, "seq", None),
        P("dp", None),
        P("dp", None),
        P(),
    )
    return jax.shard_map(
        shards, mesh=mesh, in_specs=placed, out_specs=P("dp", "seq", None), check_vma=False
    )
```

profile of v0, /device:TPU:0, one launch (start us, length us, event | category | flops | bytes accessed | tf_op | source)
XLA Modules:
  0.0 254.0 jit_solution(1753289735646659849)
XLA Ops:
  8.2 1.5 copy.57
  11.5 1.3 fusion.47
  12.9 8.1 %all-to-all-start = ((bf16[128,16,256]{0,2,1:T(8,128)(2,1)}), bf16[128,16,256]{0,2,1:T(8,128)(2,1)S(1)}, u32[]{:S(2)}, u32[]{:S(2)}) async-start(bf16[128,16,256]{0,2,1:T(8,128)(2,1)} %fusion.47), calls=%async_computation | async-start | bytes 2097152 | tf_op jit(solution)/shard_map/all_to_all | solution.py:95
  23.3 37.9 %all-gather.2.cloned.1.call-done = bf16[8,2,256,1024]{3,2,1,0:T(8,128)(2,1)} async-done(((bf16[1,2,256,1024]{3,2,1,0:T(8,128)(2,1)}), bf16[8,2,256,1024]{3,2,1,0:T(8,128)(2,1)}) %all-gather.2.cloned.1.call-update) | async-done | bytes 8388624 | tf_op jit(solution)/shard_map/all_gather | solution.py:101
  61.3 1.3 dynamic-slice_select_fusion
  63.5 3.0 %broadcast_in_dim.19 = bf16[2,256,8,2,128]{1,0,4,3,2:T(2,128)(2,1)} broadcast(bf16[2,256,8,128]{1,0,3,2:T(2,128)(2,1)S(1)} %bitcast.98), dimensions={0,1,2,4} | broadcast | bytes 3145728 | tf_op jit(solution)/shard_map/broadcast_in_dim | solution.py:108
  66.5 7.0 %all-to-all-start.1 = ((bf16[2,256,2048]{1,0,2:T(2,128)(2,1)}), bf16[2,256,2048]{1,0,2:T(2,128)(2,1)S(1)}, u32[]{:S(2)}, u32[]{:S(2)}) async-start(bf16[2,256,2048]{1,0,2:T(2,128)(2,1)} %bitcast.93), calls=%async_computation.1 | async-start | bytes 4194304 | tf_op jit(solution)/shard_map/all_to_all | solution.py:111
  76.9 30.1 %all-to-all-done.1 = bf16[2,256,2048]{1,0,2:T(2,128)(2,1)S(1)} async-done(((bf16[2,256,2048]{1,0,2:T(2,128)(2,1)}), bf16[2,256,2048]{1,0,2:T(2,128)(2,1)S(1)}, u32[]{:S(2)}, u32[]{:S(2)}) %all-to-all-start.1) | async-done | bytes 2097184 | tf_op jit(solution)/shard_map/all_to_all | solution.py:111
  106.9 1.9 broadcast_in_dim.20
  108.8 4.2 %all-to-all-start.2 = ((bf16[128,16,128]{2,0,1:T(8,128)(2,1)}), bf16[128,16,128]{2,0,1:T(8,128)(2,1)}, u32[]{:S(2)}, u32[]{:S(2)}) async-start(bf16[128,16,128]{2,0,1:T(8,128)(2,1)} %bitcast.102), calls=%async_computation.2 | async-start | bytes 1048576 | tf_op jit(solution)/shard_map/all_to_all | solution.py:96
  113.3 1.3 copy.60
  114.8 1.1 fusion.58
  116.6 1.6 copy.67
  118.2 5.9 %all-to-all-done.2 = bf16[128,16,128]{2,0,1:T(8,128)(2,1)} async-done(((bf16[128,16,128]{2,0,1:T(8,128)(2,1)}), bf16[128,16,128]{2,0,1:T(8,128)(2,1)}, u32[]{:S(2)}, u32[]{:S(2)}) %all-to-all-start.2) | async-done | bytes 524320 | tf_op jit(solution)/shard_map/all_to_all | solution.py:96
  125.1 3.6 %all-to-all-start.3 = ((bf16[128,16,128]{2,0,1:T(8,128)(2,1)}), bf16[128,16,128]{2,0,1:T(8,128)(2,1)S(1)}, u32[]{:S(2)}, u32[]{:S(2)}) async-start(bf16[128,16,128]{2,0,1:T(8,128)(2,1)} %bitcast.21), calls=%async_computation.3 | async-start | bytes 1048576 | tf_op jit(solution)/shard_map/all_to_all | solution.py:97
  128.7 2.3 pad_maximum_fusion
  131.0 8.0 %all-to-all-done.3 = bf16[128,16,128]{2,0,1:T(8,128)(2,1)S(1)} async-done(((bf16[128,16,128]{2,0,1:T(8,128)(2,1)}), bf16[128,16,128]{2,0,1:T(8,128)(2,1)S(1)}, u32[]{:S(2)}, u32[]{:S(2)}) %all-to-all-start.3) | async-done | bytes 524320 | tf_op jit(solution)/shard_map/all_to_all | solution.py:97
  139.0 87.5 %while.11 = (s32[]{:T(128)}, bf16[4,512,256]{2,1,0:T(8,128)(2,1)}, s32[4]{0:T(128)S(1)}, f32[2048,16]{0,1:T(8,128)S(1)}, bf16[2048,256]{1,0:T(8,128)(2,1)}, /*in...) while((s32[]{:T(128)}, bf16[4,512,256]{2,1,0:T(8,128)(2,1)}, ...), condition=%wide.region_10.11_spmd.clone, body=%wide.region_5.10_spmd.clone.sunk | while | flops 3470588416 | bytes 93389528 | solution.py:174
  140.4 5.0 %fusion.86 = pred[512,2048]{1,0:T(32,128)(4,1)S(1)} fusion(s32[512]{0:T(512)S(1)} %iota_add_fusion.2, s32[2048]{0:T(1024)S(1)} %get-tuple-element.197, f32[2048,16]{0,1:T(8,128)S(1)} %get-tuple-element.193, s32[]{:T(128)S(6)} %select_n.46), kind=kOutput, calls=%fused_computation.15.clone.1 | convolution fusion | flops 204537856 | bytes 1091588 | tf_op jit(solution)/shard_map/while/body/eval_jaxpr/dot_general | solution.py:133
  145.4 3.1 %fusion.90 = (f32[512]{0:T(512)S(1)}, f32[512,6144]{1,0:T(8,128)S(1)}) fusion(bf16[6144,1,128]{2,0,1:T(8,128)(2,1)S(1)} %copy-done, bf16[2048,256]{1,0:T(8,128)(2,1)} %get-tuple-element.194, s32[]{:T(128)S(6)} %select_n.46, pred[512,2048]{1,0:T(32,128)(4,1)S(1)} %fusion.86), kind=kOutput, calls=%fused_computation.73.clone.1 | convolution fusion | flops 814743040 | bytes 15337476 | tf_op jit(solution)/shard_map/while/body/eval_jaxpr/qd,kd->qk/dot_general | solution.py:154
  148.5 1.9 fusion.91
  150.4 2.4 fusion.92
  152.8 3.1 %fusion.87 = (f32[512]{0:T(512)S(1)}, f32[512,6144]{1,0:T(8,128)S(1)}) fusion(bf16[6144,1,128]{2,0,1:T(8,128)(2,1)S(1)} %copy-done, bf16[2048,256]{1,0:T(8,128)(2,1)} %get-tuple-element.194, s32[]{:T(128)S(6)} %select_n.46, pred[512,2048]{1,0:T(32,128)(4,1)S(1)} %fusion.86), kind=kOutput, calls=%fused_computation.72.clone.1 | convolution fusion | flops 814743040 | bytes 15337476 | tf_op jit(solution)/shard_map/while/body/eval_jaxpr/qd,kd->qk/dot_general | solution.py:154
  155.9 1.9 fusion.88
  157.8 2.4 fusion.89
  162.2 5.0 %fusion.86 = pred[512,2048]{1,0:T(32,128)(4,1)S(1)} fusion(s32[512]{0:T(512)S(1)} %iota_add_fusion.2, s32[2048]{0:T(1024)S(1)} %get-tuple-element.197, f32[2048,16]{0,1:T(8,128)S(1)} %get-tuple-element.193, s32[]{:T(128)S(6)} %select_n.46), kind=kOutput, calls=%fused_computation.15.clone.1 | convolution fusion | flops 204537856 | bytes 1091588 | tf_op jit(solution)/shard_map/while/body/eval_jaxpr/dot_general | solution.py:133
  167.2 3.1 %fusion.90 = (f32[512]{0:T(512)S(1)}, f32[512,6144]{1,0:T(8,128)S(1)}) fusion(bf16[6144,1,128]{2,0,1:T(8,128)(2,1)S(1)} %copy-done, bf16[2048,256]{1,0:T(8,128)(2,1)} %get-tuple-element.194, s32[]{:T(128)S(6)} %select_n.46, pred[512,2048]{1,0:T(32,128)(4,1)S(1)} %fusion.86), kind=kOutput, calls=%fused_computation.73.clone.1 | convolution fusion | flops 814743040 | bytes 15337476 | tf_op jit(solution)/shard_map/while/body/eval_jaxpr/qd,kd->qk/dot_general | solution.py:154
  170.4 1.9 fusion.91
  172.3 2.4 fusion.92
  174.6 3.1 %fusion.87 = (f32[512]{0:T(512)S(1)}, f32[512,6144]{1,0:T(8,128)S(1)}) fusion(bf16[6144,1,128]{2,0,1:T(8,128)(2,1)S(1)} %copy-done, bf16[2048,256]{1,0:T(8,128)(2,1)} %get-tuple-element.194, s32[]{:T(128)S(6)} %select_n.46, pred[512,2048]{1,0:T(32,128)(4,1)S(1)} %fusion.86), kind=kOutput, calls=%fused_computation.72.clone.1 | convolution fusion | flops 814743040 | bytes 15337476 | tf_op jit(solution)/shard_map/while/body/eval_jaxpr/qd,kd->qk/dot_general | solution.py:154
  177.7 1.9 fusion.88
  179.6 2.4 fusion.89
  184.0 5.0 %fusion.86 = pred[512,2048]{1,0:T(32,128)(4,1)S(1)} fusion(s32[512]{0:T(512)S(1)} %iota_add_fusion.2, s32[2048]{0:T(1024)S(1)} %get-tuple-element.197, f32[2048,16]{0,1:T(8,128)S(1)} %get-tuple-element.193, s32[]{:T(128)S(6)} %select_n.46), kind=kOutput, calls=%fused_computation.15.clone.1 | convolution fusion | flops 204537856 | bytes 1091588 | tf_op jit(solution)/shard_map/while/body/eval_jaxpr/dot_general | solution.py:133
  189.1 3.1 %fusion.90 = (f32[512]{0:T(512)S(1)}, f32[512,6144]{1,0:T(8,128)S(1)}) fusion(bf16[6144,1,128]{2,0,1:T(8,128)(2,1)S(1)} %copy-done, bf16[2048,256]{1,0:T(8,128)(2,1)} %get-tuple-element.194, s32[]{:T(128)S(6)} %select_n.46, pred[512,2048]{1,0:T(32,128)(4,1)S(1)} %fusion.86), kind=kOutput, calls=%fused_computation.73.clone.1 | convolution fusion | flops 814743040 | bytes 15337476 | tf_op jit(solution)/shard_map/while/body/eval_jaxpr/qd,kd->qk/dot_general | solution.py:154
  192.2 1.9 fusion.91
  194.1 2.4 fusion.92
  196.4 3.1 %fusion.87 = (f32[512]{0:T(512)S(1)}, f32[512,6144]{1,0:T(8,128)S(1)}) fusion(bf16[6144,1,128]{2,0,1:T(8,128)(2,1)S(1)} %copy-done, bf16[2048,256]{1,0:T(8,128)(2,1)} %get-tuple-element.194, s32[]{:T(128)S(6)} %select_n.46, pred[512,2048]{1,0:T(32,128)(4,1)S(1)} %fusion.86), kind=kOutput, calls=%fused_computation.72.clone.1 | convolution fusion | flops 814743040 | bytes 15337476 | tf_op jit(solution)/shard_map/while/body/eval_jaxpr/qd,kd->qk/dot_general | solution.py:154
  199.6 1.9 fusion.88
  201.4 2.4 fusion.89
  205.9 5.0 %fusion.86 = pred[512,2048]{1,0:T(32,128)(4,1)S(1)} fusion(s32[512]{0:T(512)S(1)} %iota_add_fusion.2, s32[2048]{0:T(1024)S(1)} %get-tuple-element.197, f32[2048,16]{0,1:T(8,128)S(1)} %get-tuple-element.193, s32[]{:T(128)S(6)} %select_n.46), kind=kOutput, calls=%fused_computation.15.clone.1 | convolution fusion | flops 204537856 | bytes 1091588 | tf_op jit(solution)/shard_map/while/body/eval_jaxpr/dot_general | solution.py:133
  210.9 3.1 %fusion.90 = (f32[512]{0:T(512)S(1)}, f32[512,6144]{1,0:T(8,128)S(1)}) fusion(bf16[6144,1,128]{2,0,1:T(8,128)(2,1)S(1)} %copy-done, bf16[2048,256]{1,0:T(8,128)(2,1)} %get-tuple-element.194, s32[]{:T(128)S(6)} %select_n.46, pred[512,2048]{1,0:T(32,128)(4,1)S(1)} %fusion.86), kind=kOutput, calls=%fused_computation.73.clone.1 | convolution fusion | flops 814743040 | bytes 15337476 | tf_op jit(solution)/shard_map/while/body/eval_jaxpr/qd,kd->qk/dot_general | solution.py:154
  214.0 1.9 fusion.91
  215.9 2.4 fusion.92
  218.3 3.1 %fusion.87 = (f32[512]{0:T(512)S(1)}, f32[512,6144]{1,0:T(8,128)S(1)}) fusion(bf16[6144,1,128]{2,0,1:T(8,128)(2,1)S(1)} %copy-done, bf16[2048,256]{1,0:T(8,128)(2,1)} %get-tuple-element.194, s32[]{:T(128)S(6)} %select_n.46, pred[512,2048]{1,0:T(32,128)(4,1)S(1)} %fusion.86), kind=kOutput, calls=%fused_computation.72.clone.1 | convolution fusion | flops 814743040 | bytes 15337476 | tf_op jit(solution)/shard_map/while/body/eval_jaxpr/qd,kd->qk/dot_general | solution.py:154
  221.4 1.9 fusion.88
  223.3 2.4 fusion.89
  226.5 18.7 %all_to_all.79 = bf16[16,128,256]{2,1,0:T(8,128)(2,1)S(1)} all-to-all(bf16[16,128,256]{2,1,0:T(8,128)(2,1)} %bitcast.105), channel_id=1, replica_groups=mesh['dp'=8,'seq'=16] {'seq'}, dimensions={0} | all-to-all | bytes 2097152 | tf_op jit(solution)/shard_map/all_to_all | solution.py:176
  245.9 1.3 copy.71
  (82 shorter events, 16.9 us)
Async XLA Ops:
  6.5 4.2 %copy-start.6 = (f32[64]{0:T(128)S(1)}, f32[64]{0:T(128)}, u32[]{:S(2)}) copy-start(f32[64]{0:T(128)} %constant.76.clone) | copy-start | bytes 772
  6.5 4.0 %copy-start.5 = (s32[1,2048]{1,0:T(1,128)S(1)}, s32[1,2048]{1,0:T(1,128)}, u32[]{:S(2)}) copy-start(s32[1,2048]{1,0:T(1,128)} %param.15) | copy-start | bytes 24580
  6.5 3.3 %copy-start.7 = (s32[1,16]{1,0:T(1,128)S(1)}, s32[1,16]{1,0:T(1,128)}, u32[]{:S(2)}) copy-start(s32[1,16]{1,0:T(1,128)} %param.16) | copy-start | bytes 196
  6.5 54.7 %all-gather.2.cloned.1.call-start = ((), (), s32[]{:S(2)}) async-start(), calls=%async_computation.5 | async-start | bytes 9437184 | tf_op jit(solution)/shard_map/all_gather | solution.py:101
  11.5 9.5 %copy-start.8 = (s32[8]{0:T(128)S(1)}, s32[8]{0:T(128)}, u32[]{:S(2)}) copy-start(s32[8]{0:T(128)} %param.17) | copy-start | bytes 100
  12.9 50.6 %all-to-all-start = ((bf16[128,16,256]{0,2,1:T(8,128)(2,1)}), bf16[128,16,256]{0,2,1:T(8,128)(2,1)S(1)}, u32[]{:S(2)}, u32[]{:S(2)}) async-start(bf16[128,16,256]{0,2,1:T(8,128)(2,1)} %fusion.47), calls=%async_computation | async-start | bytes 2097152 | tf_op jit(solution)/shard_map/all_to_all | solution.py:95
  63.5 11.4 %copy-start.1 = (bf16[1,128,1024]{2,1,0:T(8,128)(2,1)S(1)}, bf16[1,128,1024]{2,1,0:T(8,128)(2,1)}, u32[]{:S(2)}) copy-start(bf16[1,128,1024]{2,1,0:T(8,128)(2,1)} %param.12) | copy-start | bytes 786436
  66.5 40.5 %all-to-all-start.1 = ((bf16[2,256,2048]{1,0,2:T(2,128)(2,1)}), bf16[2,256,2048]{1,0,2:T(2,128)(2,1)S(1)}, u32[]{:S(2)}, u32[]{:S(2)}) async-start(bf16[2,256,2048]{1,0,2:T(2,128)(2,1)} %bitcast.93), calls=%async_computation.1 | async-start | bytes 4194304 | tf_op jit(solution)/shard_map/all_to_all | solution.py:111
  74.2 1.1 copy-start.2
  74.9 0.8 copy-start.3
  74.9 1.8 copy-start.4
  108.8 15.4 %all-to-all-start.2 = ((bf16[128,16,128]{2,0,1:T(8,128)(2,1)}), bf16[128,16,128]{2,0,1:T(8,128)(2,1)}, u32[]{:S(2)}, u32[]{:S(2)}) async-start(bf16[128,16,128]{2,0,1:T(8,128)(2,1)} %bitcast.102), calls=%async_computation.2 | async-start | bytes 1048576 | tf_op jit(solution)/shard_map/all_to_all | solution.py:96
  125.1 13.8 %all-to-all-start.3 = ((bf16[128,16,128]{2,0,1:T(8,128)(2,1)}), bf16[128,16,128]{2,0,1:T(8,128)(2,1)S(1)}, u32[]{:S(2)}, u32[]{:S(2)}) async-start(bf16[128,16,128]{2,0,1:T(8,128)(2,1)} %bitcast.21), calls=%async_computation.3 | async-start | bytes 1048576 | tf_op jit(solution)/shard_map/all_to_all | solution.py:97
  140.4 5.0 %copy-start = (bf16[6144,1,128]{2,0,1:T(8,128)(2,1)S(1)}, bf16[6144,1,128]{2,0,1:T(8,128)(2,1)}, u32[]{:S(2)}) copy-start(bf16[6144,1,128]{2,0,1:T(8,128)(2,1)} %get-tuple-element.195) | copy-start | bytes 4718596 | tf_op jit(solution)/shard_map/while
  162.2 5.0 %copy-start = (bf16[6144,1,128]{2,0,1:T(8,128)(2,1)S(1)}, bf16[6144,1,128]{2,0,1:T(8,128)(2,1)}, u32[]{:S(2)}) copy-start(bf16[6144,1,128]{2,0,1:T(8,128)(2,1)} %get-tuple-element.195) | copy-start | bytes 4718596 | tf_op jit(solution)/shard_map/while
  184.0 5.0 %copy-start = (bf16[6144,1,128]{2,0,1:T(8,128)(2,1)S(1)}, bf16[6144,1,128]{2,0,1:T(8,128)(2,1)}, u32[]{:S(2)}) copy-start(bf16[6144,1,128]{2,0,1:T(8,128)(2,1)} %get-tuple-element.195) | copy-start | bytes 4718596 | tf_op jit(solution)/shard_map/while
  205.9 5.0 %copy-start = (bf16[6144,1,128]{2,0,1:T(8,128)(2,1)S(1)}, bf16[6144,1,128]{2,0,1:T(8,128)(2,1)}, u32[]{:S(2)}) copy-start(bf16[6144,1,128]{2,0,1:T(8,128)(2,1)} %get-tuple-element.195) | copy-start | bytes 4718596 | tf_op jit(solution)/shard_map/while
Sparse Core Ops, SparseCore 0:
  9.1 52.1 all-gather.1
where the time goes:
time: 255 us; the launch traced here: 254 us
  waiting for transfers between devices  82.6 us (32%)
  matrix products  64.6 us (25%)
  local copies, waits for them, and re-layouts  24.6 us (10%)
  starting transfers between devices  22.9 us (9%)
  other arithmetic  22.4 us (9%)
  blocking collectives  18.7 us (7%)
  between operations  15.4 us (6%)
  loops' own time  2.79 us (1%)
    all_gather x1, waiting for transfers between devices, shards(): incoming = lax.all_gather(stem_kv, 'dp', axis=0, tiled=True)  37.9 us
    all_to_all x1, waiting for transfers between devices, shards(): lax.all_to_all(stem_wide, 'seq', split_axis=2, concat_axis=1, tiled=True)  30.1 us
    dot_general x8, matrix products, block_out(): jnp.einsum('qd,kd->qk', query_rows, key_sets[:, kv_head], preferred_eleme...  24.9 us
    dot_general x4, matrix products, block_out(): jnp.dot(reach_block, onehot.T, precision=lax.Precision.HIGHEST, preferred...  20 us
    dot_general x8, matrix products, block_out(): jnp.dot(exp_scores.astype(jnp.bfloat16), value_sets[:, kv_head], preferre...  18.8 us
    all_to_all x1, blocking collectives, shards(): lax.all_to_all(as_sent(attended_heads), 'seq', split_axis=0, concat_axis=...  18.7 us
    reduce_sum x8, other arithmetic, block_out(): totals = jnp.sum(exp_scores, axis=1, keepdims=True)  15.1 us
    all_to_all x1, starting transfers between devices, shards(): lax.all_to_all(q_rot, 'seq', split_axis=1, concat_axis=0, tiled=True)  8.13 us
  transfers between devices with their start and end apart: 5, of which 4 were waited for; matrix products, arithmetic and copies ran while one was open for 7% of the time, Pallas kernels for 0%

commit v1 on v0

--- a/solution.py
+++ b/solution.py
@@ -98,7 +98,9 @@
     )
     owner_group = lax.dynamic_index_in_dim(stem_owner, lax.axis_index("dp"), 0, keepdims=False)
     empty_block = jnp.zeros(stem_kv.shape[1:], jnp.bfloat16)
-    incoming = lax.all_gather(stem_kv, "dp", axis=0, tiled=True)
+    incoming = jnp.concatenate(
+        lax.all_to_all(jnp.stack([stem_kv] * lax.axis_size("dp")), "dp", 0, 0), axis=0
+    )
     inside = (owner_group >= 0) & (owner_group < incoming.shape[0])
     chosen = lax.dynamic_index_in_dim(
         incoming, jnp.clip(owner_group, 0, incoming.shape[0] - 1), 0, keepdims=False

time: 255 us -> 309 us (1.21)
  waiting for transfers between devices: 82.6 us -> 143 us
  between operations: 15.4 us -> 2 us
  local copies, waits for them, and re-layouts: 24.6 us -> 30.8 us
    all_to_all x0 -> x1, waiting for transfers between devices: none -> 90.6 us  [shards(): lax.all_to_all(jnp.stack([stem_kv] * lax.axis_size('dp')), 'dp', 0, 0)]
    all_gather x1 -> x0, waiting for transfers between devices: 37.9 us -> none  [shards(): incoming = lax.all_gather(stem_kv, 'dp', axis=0, tiled=True)]
    all_to_all x1, waiting for transfers between devices: 0.01 us -> 13 us  [shards(): lax.all_to_all(q_rot, 'seq', split_axis=1, concat_axis=0, tiled=True)]
    another operation x1 -> x3, local copies, waits for them, and re-layouts: 0.09 us -> 8.14 us  [the longest x1 5.54 us: shards(): jnp.stack([stem_kv] * lax.axis_size('dp'))]
    all_to_all x0 -> x1, starting transfers between devices: none -> 5.08 us  [shards(): lax.all_to_all(jnp.stack([stem_kv] * lax.axis_size('dp')), 'dp', 0, 0)]
    all_to_all x1, waiting for transfers between devices: 30.1 us -> 25.8 us  [shards(): lax.all_to_all(stem_wide, 'seq', split_axis=2, concat_axis=1, tiled=True)]
    all_to_all x1, starting transfers between devices: 6.98 us -> 3.72 us  [shards(): lax.all_to_all(stem_wide, 'seq', split_axis=2, concat_axis=1, tiled=True)]
  transfers between devices with their start and end apart: 5 -> 5, of which waited for: 4 -> 5; matrix products, arithmetic and copies ran while one was open for 7% -> 5% of each run, Pallas kernels for 0% -> 0%
where the time goes in v1:
time: 309 us; the launch traced here: 308 us
  waiting for transfers between devices  143 us (46%)
  matrix products  64.6 us (21%)
  local copies, waits for them, and re-layouts  30.8 us (10%)
  starting transfers between devices  24.7 us (8%)
  other arithmetic  22.4 us (7%)
  blocking collectives  18 us (6%)
    all_to_all x1, waiting for transfers between devices, shards(): lax.all_to_all(jnp.stack([stem_kv] * lax.axis_size('dp')), 'dp', 0, 0)  90.6 us
    all_to_all x1, waiting for transfers between devices, shards(): lax.all_to_all(stem_wide, 'seq', split_axis=2, concat_axis=1, tiled=True)  25.8 us
    dot_general x8, matrix products, block_out(): jnp.einsum('qd,kd->qk', query_rows, key_sets[:, kv_head], preferred_eleme...  24.9 us
    dot_general x4, matrix products, block_out(): jnp.dot(reach_block, onehot.T, precision=lax.Precision.HIGHEST, preferred...  20 us
    dot_general x8, matrix products, block_out(): jnp.dot(exp_scores.astype(jnp.bfloat16), value_sets[:, kv_head], preferre...  18.8 us
    all_to_all x1, blocking collectives, shards(): lax.all_to_all(as_sent(attended_heads), 'seq', split_axis=0, concat_axis=...  18 us
    reduce_sum x8, other arithmetic, block_out(): totals = jnp.sum(exp_scores, axis=1, keepdims=True)  15.1 us
    all_to_all x1, waiting for transfers between devices, shards(): lax.all_to_all(q_rot, 'seq', split_axis=1, concat_axis=0, tiled=True)  13 us
  transfers between devices with their start and end apart: 5, of which 5 were waited for; matrix products, arithmetic and copies ran while one was open for 5% of the time, Pallas kernels for 0%

profile of v1, /device:TPU:0, one launch (start us, length us, event | category | flops | bytes accessed | tf_op | source)
XLA Modules:
  0.0 308.1 jit_solution(10072991919857219775)
XLA Ops:
  0.0 2.5 copy.61
  2.5 5.5 %stack.2 = bf16[8,1,2,256,1024]{3,2,4,1,0:T(2,128)(2,1)} broadcast(bf16[2,256,1024]{1,0,2:T(2,128)(2,1)S(1)} %copy.61), dimensions={2,3,4} | broadcast | bytes 9437184 | tf_op jit(solution)/shard_map/stack | solution.py:102
  8.1 5.1 %all-to-all-start.1 = ((bf16[8,1,2,256,1024]{3,2,4,1,0:T(2,128)(2,1)}), bf16[8,1,2,256,1024]{3,2,4,1,0:T(2,128)(2,1)}, u32[]{:S(2)}, u32[]{:S(2)}) async-start(bf16[8,1,2,256,1024]{3,2,4,1,0:T(2,128)(2,1)} %stack.2), calls=%async_computation.1 | async-start | bytes 16777216 | tf_op jit(solution)/shard_map/all_to_all | solution.py:102
  15.8 1.3 fusion.47
  17.1 90.6 %all-to-all-done.1 = bf16[8,1,2,256,1024]{3,2,4,1,0:T(2,128)(2,1)} async-done(((bf16[8,1,2,256,1024]{3,2,4,1,0:T(2,128)(2,1)}), bf16[8,1,2,256,1024]{3,2,4,1,0:T(2,128)(2,1)}, u32[]{:S(2)}, u32[]{:S(2)}) %all-to-all-start.1) | async-done | bytes 8388640 | tf_op jit(solution)/shard_map/all_to_all | solution.py:102
  107.8 8.1 %all-to-all-start = ((bf16[128,16,256]{0,2,1:T(8,128)(2,1)}), bf16[128,16,256]{0,2,1:T(8,128)(2,1)S(1)}, u32[]{:S(2)}, u32[]{:S(2)}) async-start(bf16[128,16,256]{0,2,1:T(8,128)(2,1)} %fusion.47), calls=%async_computation | async-start | bytes 2097152 | tf_op jit(solution)/shard_map/all_to_all | solution.py:95
  118.2 2.1 broadcast_select_fusion
  120.3 13.0 %all-to-all-done = bf16[128,16,256]{0,2,1:T(8,128)(2,1)S(1)} async-done(((bf16[128,16,256]{0,2,1:T(8,128)(2,1)}), bf16[128,16,256]{0,2,1:T(8,128)(2,1)S(1)}, u32[]{:S(2)}, u32[]{:S(2)}) %all-to-all-start) | async-done | bytes 1048608 | tf_op jit(solution)/shard_map/all_to_all | solution.py:95
  133.3 3.0 broadcast_in_dim.19
  136.3 3.7 %all-to-all-start.2 = ((bf16[2,256,2048]{1,0,2:T(2,128)(2,1)}), bf16[2,256,2048]{1,0,2:T(2,128)(2,1)S(1)}, u32[]{:S(2)}, u32[]{:S(2)}) async-start(bf16[2,256,2048]{1,0,2:T(2,128)(2,1)} %bitcast.94), calls=%async_computation.2 | async-start | bytes 4194304 | tf_op jit(solution)/shard_map/all_to_all | solution.py:113
  143.4 25.8 %all-to-all-done.2 = bf16[2,256,2048]{1,0,2:T(2,128)(2,1)S(1)} async-done(((bf16[2,256,2048]{1,0,2:T(2,128)(2,1)}), bf16[2,256,2048]{1,0,2:T(2,128)(2,1)S(1)}, u32[]{:S(2)}, u32[]{:S(2)}) %all-to-all-start.2) | async-done | bytes 2097184 | tf_op jit(solution)/shard_map/all_to_all | solution.py:113
  169.2 1.9 broadcast_in_dim.20
  171.0 4.2 %all-to-all-start.3 = ((bf16[128,16,128]{2,0,1:T(8,128)(2,1)}), bf16[128,16,128]{2,0,1:T(8,128)(2,1)}, u32[]{:S(2)}, u32[]{:S(2)}) async-start(bf16[128,16,128]{2,0,1:T(8,128)(2,1)} %bitcast.103), calls=%async_computation.3 | async-start | bytes 1048576 | tf_op jit(solution)/shard_map/all_to_all | solution.py:96
  178.9 1.6 copy.67
  180.5 5.4 %all-to-all-done.3 = bf16[128,16,128]{2,0,1:T(8,128)(2,1)} async-done(((bf16[128,16,128]{2,0,1:T(8,128)(2,1)}), bf16[128,16,128]{2,0,1:T(8,128)(2,1)}, u32[]{:S(2)}, u32[]{:S(2)}) %all-to-all-start.3) | async-done | bytes 524320 | tf_op jit(solution)/shard_map/all_to_all | solution.py:96
  186.8 3.6 %all-to-all-start.4 = ((bf16[128,16,128]{2,0,1:T(8,128)(2,1)}), bf16[128,16,128]{2,0,1:T(8,128)(2,1)S(1)}, u32[]{:S(2)}, u32[]{:S(2)}) async-start(bf16[128,16,128]{2,0,1:T(8,128)(2,1)} %bitcast.22), calls=%async_computation.4 | async-start | bytes 1048576 | tf_op jit(solution)/shard_map/all_to_all | solution.py:97
  190.4 2.3 pad_maximum_fusion
  192.7 7.8 %all-to-all-done.4 = bf16[128,16,128]{2,0,1:T(8,128)(2,1)S(1)} async-done(((bf16[128,16,128]{2,0,1:T(8,128)(2,1)}), bf16[128,16,128]{2,0,1:T(8,128)(2,1)S(1)}, u32[]{:S(2)}, u32[]{:S(2)}) %all-to-all-start.4) | async-done | bytes 524320 | tf_op jit(solution)/shard_map/all_to_all | solution.py:97
  200.6 87.5 %while.11 = (s32[]{:T(128)}, bf16[4,512,256]{2,1,0:T(8,128)(2,1)}, s32[4]{0:T(128)S(1)}, f32[2048,16]{0,1:T(8,128)S(1)}, bf16[2048,256]{1,0:T(8,128)(2,1)}, /*in...) while((s32[]{:T(128)}, bf16[4,512,256]{2,1,0:T(8,128)(2,1)}, ...), condition=%wide.region_10.11_spmd.clone, body=%wide.region_5.10_spmd.clone.sunk | while | flops 3470588416 | bytes 93389528 | solution.py:176
  202.0 5.0 %fusion.86 = pred[512,2048]{1,0:T(32,128)(4,1)S(1)} fusion(s32[512]{0:T(512)S(1)} %iota_add_fusion.2, s32[2048]{0:T(1024)S(1)} %get-tuple-element.197, f32[2048,16]{0,1:T(8,128)S(1)} %get-tuple-element.193, s32[]{:T(128)S(6)} %select_n.46), kind=kOutput, calls=%fused_computation.15.clone.1 | convolution fusion | flops 204537856 | bytes 1091588 | tf_op jit(solution)/shard_map/while/body/eval_jaxpr/dot_general | solution.py:135
  207.0 3.1 %fusion.90 = (f32[512]{0:T(512)S(1)}, f32[512,6144]{1,0:T(8,128)S(1)}) fusion(bf16[6144,1,128]{2,0,1:T(8,128)(2,1)S(1)} %copy-done, bf16[2048,256]{1,0:T(8,128)(2,1)} %get-tuple-element.194, s32[]{:T(128)S(6)} %select_n.46, pred[512,2048]{1,0:T(32,128)(4,1)S(1)} %fusion.86), kind=kOutput, calls=%fused_computation.73.clone.1 | convolution fusion | flops 814743040 | bytes 15337476 | tf_op jit(solution)/shard_map/while/body/eval_jaxpr/qd,kd->qk/dot_general | solution.py:156
  210.1 1.9 fusion.91
  212.0 2.4 fusion.92
  214.4 3.1 %fusion.87 = (f32[512]{0:T(512)S(1)}, f32[512,6144]{1,0:T(8,128)S(1)}) fusion(bf16[6144,1,128]{2,0,1:T(8,128)(2,1)S(1)} %copy-done, bf16[2048,256]{1,0:T(8,128)(2,1)} %get-tuple-element.194, s32[]{:T(128)S(6)} %select_n.46, pred[512,2048]{1,0:T(32,128)(4,1)S(1)} %fusion.86), kind=kOutput, calls=%fused_computation.72.clone.1 | convolution fusion | flops 814743040 | bytes 15337476 | tf_op jit(solution)/shard_map/while/body/eval_jaxpr/qd,kd->qk/dot_general | solution.py:156
  217.5 1.9 fusion.88
  219.4 2.4 fusion.89
  223.8 5.0 %fusion.86 = pred[512,2048]{1,0:T(32,128)(4,1)S(1)} fusion(s32[512]{0:T(512)S(1)} %iota_add_fusion.2, s32[2048]{0:T(1024)S(1)} %get-tuple-element.197, f32[2048,16]{0,1:T(8,128)S(1)} %get-tuple-element.193, s32[]{:T(128)S(6)} %select_n.46), kind=kOutput, calls=%fused_computation.15.clone.1 | convolution fusion | flops 204537856 | bytes 1091588 | tf_op jit(solution)/shard_map/while/body/eval_jaxpr/dot_general | solution.py:135
  228.8 3.1 %fusion.90 = (f32[512]{0:T(512)S(1)}, f32[512,6144]{1,0:T(8,128)S(1)}) fusion(bf16[6144,1,128]{2,0,1:T(8,128)(2,1)S(1)} %copy-done, bf16[2048,256]{1,0:T(8,128)(2,1)} %get-tuple-element.194, s32[]{:T(128)S(6)} %select_n.46, pred[512,2048]{1,0:T(32,128)(4,1)S(1)} %fusion.86), kind=kOutput, calls=%fused_computation.73.clone.1 | convolution fusion | flops 814743040 | bytes 15337476 | tf_op jit(solution)/shard_map/while/body/eval_jaxpr/qd,kd->qk/dot_general | solution.py:156
  231.9 1.9 fusion.91
  233.8 2.4 fusion.92
  236.2 3.1 %fusion.87 = (f32[512]{0:T(512)S(1)}, f32[512,6144]{1,0:T(8,128)S(1)}) fusion(bf16[6144,1,128]{2,0,1:T(8,128)(2,1)S(1)} %copy-done, bf16[2048,256]{1,0:T(8,128)(2,1)} %get-tuple-element.194, s32[]{:T(128)S(6)} %select_n.46, pred[512,2048]{1,0:T(32,128)(4,1)S(1)} %fusion.86), kind=kOutput, calls=%fused_computation.72.clone.1 | convolution fusion | flops 814743040 | bytes 15337476 | tf_op jit(solution)/shard_map/while/body/eval_jaxpr/qd,kd->qk/dot_general | solution.py:156
  239.3 1.9 fusion.88
  241.2 2.4 fusion.89
  245.6 5.0 %fusion.86 = pred[512,2048]{1,0:T(32,128)(4,1)S(1)} fusion(s32[512]{0:T(512)S(1)} %iota_add_fusion.2, s32[2048]{0:T(1024)S(1)} %get-tuple-element.197, f32[2048,16]{0,1:T(8,128)S(1)} %get-tuple-element.193, s32[]{:T(128)S(6)} %select_n.46), kind=kOutput, calls=%fused_computation.15.clone.1 | convolution fusion | flops 204537856 | bytes 1091588 | tf_op jit(solution)/shard_map/while/body/eval_jaxpr/dot_general | solution.py:135
  250.6 3.1 %fusion.90 = (f32[512]{0:T(512)S(1)}, f32[512,6144]{1,0:T(8,128)S(1)}) fusion(bf16[6144,1,128]{2,0,1:T(8,128)(2,1)S(1)} %copy-done, bf16[2048,256]{1,0:T(8,128)(2,1)} %get-tuple-element.194, s32[]{:T(128)S(6)} %select_n.46, pred[512,2048]{1,0:T(32,128)(4,1)S(1)} %fusion.86), kind=kOutput, calls=%fused_computation.73.clone.1 | convolution fusion | flops 814743040 | bytes 15337476 | tf_op jit(solution)/shard_map/while/body/eval_jaxpr/qd,kd->qk/dot_general | solution.py:156
  253.8 1.9 fusion.91
  255.6 2.4 fusion.92
  258.0 3.1 %fusion.87 = (f32[512]{0:T(512)S(1)}, f32[512,6144]{1,0:T(8,128)S(1)}) fusion(bf16[6144,1,128]{2,0,1:T(8,128)(2,1)S(1)} %copy-done, bf16[2048,256]{1,0:T(8,128)(2,1)} %get-tuple-element.194, s32[]{:T(128)S(6)} %select_n.46, pred[512,2048]{1,0:T(32,128)(4,1)S(1)} %fusion.86), kind=kOutput, calls=%fused_computation.72.clone.1 | convolution fusion | flops 814743040 | bytes 15337476 | tf_op jit(solution)/shard_map/while/body/eval_jaxpr/qd,kd->qk/dot_general | solution.py:156
  261.1 1.9 fusion.88
  263.0 2.4 fusion.89
  267.4 5.0 %fusion.86 = pred[512,2048]{1,0:T(32,128)(4,1)S(1)} fusion(s32[512]{0:T(512)S(1)} %iota_add_fusion.2, s32[2048]{0:T(1024)S(1)} %get-tuple-element.197, f32[2048,16]{0,1:T(8,128)S(1)} %get-tuple-element.193, s32[]{:T(128)S(6)} %select_n.46), kind=kOutput, calls=%fused_computation.15.clone.1 | convolution fusion | flops 204537856 | bytes 1091588 | tf_op jit(solution)/shard_map/while/body/eval_jaxpr/dot_general | solution.py:135
  272.5 3.1 %fusion.90 = (f32[512]{0:T(512)S(1)}, f32[512,6144]{1,0:T(8,128)S(1)}) fusion(bf16[6144,1,128]{2,0,1:T(8,128)(2,1)S(1)} %copy-done, bf16[2048,256]{1,0:T(8,128)(2,1)} %get-tuple-element.194, s32[]{:T(128)S(6)} %select_n.46, pred[512,2048]{1,0:T(32,128)(4,1)S(1)} %fusion.86), kind=kOutput, calls=%fused_computation.73.clone.1 | convolution fusion | flops 814743040 | bytes 15337476 | tf_op jit(solution)/shard_map/while/body/eval_jaxpr/qd,kd->qk/dot_general | solution.py:156
  275.6 1.9 fusion.91
  277.5 2.4 fusion.92
  279.8 3.1 %fusion.87 = (f32[512]{0:T(512)S(1)}, f32[512,6144]{1,0:T(8,128)S(1)}) fusion(bf16[6144,1,128]{2,0,1:T(8,128)(2,1)S(1)} %copy-done, bf16[2048,256]{1,0:T(8,128)(2,1)} %get-tuple-element.194, s32[]{:T(128)S(6)} %select_n.46, pred[512,2048]{1,0:T(32,128)(4,1)S(1)} %fusion.86), kind=kOutput, calls=%fused_computation.72.clone.1 | convolution fusion | flops 814743040 | bytes 15337476 | tf_op jit(solution)/shard_map/while/body/eval_jaxpr/qd,kd->qk/dot_general | solution.py:156
  282.9 1.9 fusion.88
  284.8 2.4 fusion.89
  288.1 18.0 %all_to_all.84 = bf16[16,128,256]{2,1,0:T(8,128)(2,1)S(1)} all-to-all(bf16[16,128,256]{2,1,0:T(8,128)(2,1)} %bitcast.107), channel_id=1, replica_groups=mesh['dp'=8,'seq'=16] {'seq'}, dimensions={0} | all-to-all | bytes 2097152 | tf_op jit(solution)/shard_map/all_to_all | solution.py:178
  (84 shorter events, 18.8 us)
Async XLA Ops:
  8.1 5.1 %copy-start.6 = (s32[1,2048]{1,0:T(1,128)S(1)}, s32[1,2048]{1,0:T(1,128)}, u32[]{:S(2)}) copy-start(s32[1,2048]{1,0:T(1,128)} %param.15) | copy-start | bytes 24580
  8.1 5.3 %copy-start.1 = (bf16[1,128,4096]{2,1,0:T(8,128)(2,1)S(1)}, bf16[1,128,4096]{2,1,0:T(8,128)(2,1)}, u32[]{:S(2)}) copy-start(bf16[1,128,4096]{2,1,0:T(8,128)(2,1)} %param.11) | copy-start | bytes 3145732
  8.1 99.7 %all-to-all-start.1 = ((bf16[8,1,2,256,1024]{3,2,4,1,0:T(2,128)(2,1)}), bf16[8,1,2,256,1024]{3,2,4,1,0:T(2,128)(2,1)}, u32[]{:S(2)}, u32[]{:S(2)}) async-start(bf16[8,1,2,256,1024]{3,2,4,1,0:T(2,128)(2,1)} %stack.2), calls=%async_computation.1 | async-start | bytes 16777216 | tf_op jit(solution)/shard_map/all_to_all | solution.py:102
  13.2 0.9 copy-start.8
  13.2 1.8 copy-start.7
  15.8 100.1 %copy-start.9 = (s32[8]{0:T(128)S(1)}, s32[8]{0:T(128)}, u32[]{:S(2)}) copy-start(s32[8]{0:T(128)} %param.17) | copy-start | bytes 100
  107.8 25.6 %all-to-all-start = ((bf16[128,16,256]{0,2,1:T(8,128)(2,1)}), bf16[128,16,256]{0,2,1:T(8,128)(2,1)S(1)}, u32[]{:S(2)}, u32[]{:S(2)}) async-start(bf16[128,16,256]{0,2,1:T(8,128)(2,1)} %fusion.47), calls=%async_computation | async-start | bytes 2097152 | tf_op jit(solution)/shard_map/all_to_all | solution.py:95
  133.3 8.1 %copy-start.2 = (bf16[1,128,1024]{2,1,0:T(8,128)(2,1)S(1)}, bf16[1,128,1024]{2,1,0:T(8,128)(2,1)}, u32[]{:S(2)}) copy-start(bf16[1,128,1024]{2,1,0:T(8,128)(2,1)} %param.12) | copy-start | bytes 786436
  136.3 32.9 %all-to-all-start.2 = ((bf16[2,256,2048]{1,0,2:T(2,128)(2,1)}), bf16[2,256,2048]{1,0,2:T(2,128)(2,1)S(1)}, u32[]{:S(2)}, u32[]{:S(2)}) async-start(bf16[2,256,2048]{1,0,2:T(2,128)(2,1)} %bitcast.94), calls=%async_computation.2 | async-start | bytes 4194304 | tf_op jit(solution)/shard_map/all_to_all | solution.py:113
  140.8 1.1 copy-start.3
  141.5 0.8 copy-start.4
  141.5 1.8 copy-start.5
  171.0 14.9 %all-to-all-start.3 = ((bf16[128,16,128]{2,0,1:T(8,128)(2,1)}), bf16[128,16,128]{2,0,1:T(8,128)(2,1)}, u32[]{:S(2)}, u32[]{:S(2)}) async-start(bf16[128,16,128]{2,0,1:T(8,128)(2,1)} %bitcast.103), calls=%async_computation.3 | async-start | bytes 1048576 | tf_op jit(solution)/shard_map/all_to_all | solution.py:96
  186.8 13.7 %all-to-all-start.4 = ((bf16[128,16,128]{2,0,1:T(8,128)(2,1)}), bf16[128,16,128]{2,0,1:T(8,128)(2,1)S(1)}, u32[]{:S(2)}, u32[]{:S(2)}) async-start(bf16[128,16,128]{2,0,1:T(8,128)(2,1)} %bitcast.22), calls=%async_computation.4 | async-start | bytes 1048576 | tf_op jit(solution)/shard_map/all_to_all | solution.py:97
  202.0 5.0 %copy-start = (bf16[6144,1,128]{2,0,1:T(8,128)(2,1)S(1)}, bf16[6144,1,128]{2,0,1:T(8,128)(2,1)}, u32[]{:S(2)}) copy-start(bf16[6144,1,128]{2,0,1:T(8,128)(2,1)} %get-tuple-element.195) | copy-start | bytes 4718596 | tf_op jit(solution)/shard_map/while
  223.8 5.0 %copy-start = (bf16[6144,1,128]{2,0,1:T(8,128)(2,1)S(1)}, bf16[6144,1,128]{2,0,1:T(8,128)(2,1)}, u32[]{:S(2)}) copy-start(bf16[6144,1,128]{2,0,1:T(8,128)(2,1)} %get-tuple-element.195) | copy-start | bytes 4718596 | tf_op jit(solution)/shard_map/while
  245.6 5.0 %copy-start = (bf16[6144,1,128]{2,0,1:T(8,128)(2,1)S(1)}, bf16[6144,1,128]{2,0,1:T(8,128)(2,1)}, u32[]{:S(2)}) copy-start(bf16[6144,1,128]{2,0,1:T(8,128)(2,1)} %get-tuple-element.195) | copy-start | bytes 4718596 | tf_op jit(solution)/shard_map/while
  267.4 5.0 %copy-start = (bf16[6144,1,128]{2,0,1:T(8,128)(2,1)S(1)}, bf16[6144,1,128]{2,0,1:T(8,128)(2,1)}, u32[]{:S(2)}) copy-start(bf16[6144,1,128]{2,0,1:T(8,128)(2,1)} %get-tuple-element.195) | copy-start | bytes 4718596 | tf_op jit(solution)/shard_map/while
